TPU v7x, 512 devices: a whole 4x8x8 slice. The times are simulated.
512 devices in a mesh: cuts: 4 (over y_hi, core), mode: 128 (over x, y_lo, z).
Axes of the slice: x: 4, y: 8 (y_hi: 2, y_lo: 4; y = y_hi * 4 + y_lo), z: 8, core: 2. Of those that a mesh axis runs over, the one named last changes fastest.
Arguments:
- stem: bfloat16 [4, 2, 1024, 16384], P('cuts', None, None, 'mode'), may hold values from -6 to 6
- branches: bfloat16 [3, 2, 1024, 1024], P(None, None, None, 'mode'), may hold values from -0.125 to 0.125
- order: int32 [3], replicated, may hold values from 0 to 2, each once
- swap_order: int32 [3, 1024], replicated, may hold values from 0 to 1023, each once within a row
- row_bits: int32 [2048], replicated, may hold values from 0 to 1023
- column_bits: int32 [2048], replicated, may hold values from 0 to 16383
Outputs:
- stem_out: bfloat16 [4, 2, 1024, 16384], P('cuts', None, None, 'mode')
- amplitudes: float32 [2, 2048], P(None, ('cuts', 'mode'))
All inputs are finite; a program needn't handle non-finite values.
Results may differ from a plain program's by a relative error of at most 0.009.
Values may be sent and summed in bfloat16 or wider, within the bound.
A program may use at most 128 MiB of HBM per device.

v0:
```python
import jax
import jax.numpy as jnp
from jax import lax
from jax.sharding import Mesh
from jax.sharding import PartitionSpec as P

MODE = ("mode_0", "mode_1", "mode_2")
CUTS_MODE = ("cuts_0", "cuts_1", "mode_0", "mode_1", "mode_2")
CUTS = ("cuts_0", "cuts_1")


def cut_rows(length, count):
    unit = 8 if length >= 8 * count else 1
    return [length // unit * k // count * unit for k in range(1, count)]


def gather_in_order(shard, axes, turns):
    blocks = shard[None]
    for k in turns:
        blocks = lax.all_gather(blocks, axes[k], axis=0, tiled=True)
    held = [lax.axis_size(axes[k]) for k in reversed(turns)]
    blocks = blocks.reshape(*held, *shard.shape)
    turned = sorted(range(len(turns)), key=lambda place: turns[len(turns) - 1 - place])
    return blocks.transpose(*turned, *range(len(turns), blocks.ndim)).reshape(-1, *shard.shape)


def joined_along(blocks, dim):
    blocks = jnp.moveaxis(blocks, 0, dim)
    dims = blocks.shape
    return blocks.reshape(*dims[:dim], dims[dim] * dims[dim + 1], *dims[dim + 2 :])


def gather_at_once(shard, axes, dim):
    cut = max(range(max(1, shard.ndim - 1)), key=lambda d: shard.shape[d])
    count, finished = (len(axes), [])
    for initial, slab in enumerate(jnp.split(shard, cut_rows(shard.shape[cut], count), axis=cut)):
        if slab.size:
            turns = [(initial - k) % count for k in range(count)]
            finished.append(gather_in_order(slab, axes, turns))
    return joined_along(jnp.concatenate(finished, axis=cut + 1), dim)


def over_axes(shard, axes):
    for axis in axes:
        shard = lax.psum(shard, axis)
    return shard


def absorb(matrix, part):
    numbers = (((0,), (0,)), ((), ()))

    def product(left, right):
        return lax.dot_general(left, right, numbers, preferred_element_type=jnp.float32)

    real = product(matrix[0], part[0]) - product(matrix[1], part[1])
    imag = product(matrix[0], part[1]) + product(matrix[1], part[0])
    return jnp.stack([real, imag], axis=0)


def body(stem, branches, order, swap_order, row_bits, column_bits):
    local = stem[0]
    groups = lax.axis_size(MODE)
    width = local.shape[1]
    rows = local.shape[2]
    everything = gather_at_once(branches, MODE, 3)
    for step in range(swap_order.shape[0]):
        moved = jnp.take(local, swap_order[step], axis=1)
        view = moved.reshape(2, groups, width // groups, rows)
        swapped = lax.all_to_all(view, MODE, split_axis=1, concat_axis=1, tiled=True)
        current = swapped.reshape(2, width, rows)
        pick = order[step]
        matrix = lax.dynamic_index_in_dim(everything, pick, 0, keepdims=False)
        local = absorb(matrix, current).astype(jnp.bfloat16)
    offset = lax.axis_index(MODE) * rows
    column_local = column_bits - offset
    inside = jnp.logical_and(column_local >= 0, column_local < rows)
    flat_index = row_bits * rows + jnp.clip(column_local, 0, rows - 1)
    flat = local.reshape(2, width * rows)
    values = jnp.take(flat, flat_index, axis=1).astype(jnp.float32)
    values = jnp.where(inside[None, :], values, jnp.zeros_like(values))
    total_amps = over_axes(values, CUTS_MODE)
    share = values.shape[1] // lax.axis_size(CUTS_MODE)
    amplitudes = lax.dynamic_slice_in_dim(total_amps, lax.axis_index(CUTS_MODE) * share, share, 1)
    return (local[None], amplitudes)


def solution(mesh):
    finer = Mesh(
        mesh.devices.reshape(2, 2, 4, 4, 8), ("cuts_0", "cuts_1", "mode_0", "mode_1", "mode_2")
    )
    placed = (P(CUTS, None, None, MODE), P(None, None, None, MODE), P(), P(), P(), P())
    return jax.shard_map(
        body,
        mesh=finer,
        in_specs=placed,
        out_specs=(P(CUTS, None, None, MODE), P(None, CUTS_MODE)),
        check_vma=False,
    )
```

profile of v0, /device:TPU:4, one launch (start us, length us, event | category | flops | bytes accessed | tf_op | source)
XLA Modules:
  0.0 671.8 jit_solution(10324625984427429543)
XLA Ops:
  7.2 0.0 all-gather.12.cloned.1.call-start
  7.2 0.9 fusion.45
  8.1 33.4 %all-gather.2 = bf16[24,2,344,8]{2,3,1,0:T(8,128)(2,1)} all-gather(bf16[3,2,344,8]{2,3,1,0:T(8,128)(2,1)S(1)} %get-tuple-element.14), channel_id=4, replica_groups=mesh['cuts_0'=2,'cuts_1'=2,'mode_0'=4,'mode_1'=4,'mode_2'=8] {'mode_2'}, dimensions={0}, use_global_device_ids=true | all-gather | bytes 297216 | tf_op jit(solution)/shard_map/all_gather | solution.py:20
  41.5 0.0 all-gather.12.cloned.1.call-update
  41.6 0.0 all-gather.8.cloned.1.call-start
  41.6 0.8 split.9
  42.4 10.8 %all-gather = bf16[12,2,336,8]{2,3,1,0:T(8,128)(2,1)S(1)} all-gather(bf16[3,2,336,8]{2,3,1,0:T(8,128)(2,1)S(1)} %split.9), channel_id=2, replica_groups=mesh['cuts_0'=2,'cuts_1'=2,'mode_0'=4,'mode_1'=4,'mode_2'=8] {'mode_0'}, dimensions={0}, use_global_device_ids=true | all-gather | bytes 161280 | tf_op jit(solution)/shard_map/all_gather | solution.py:20
  53.2 29.4 %all_gather.28 = bf16[32,3,2,336,8]{3,4,2,1,0:T(8,128)(2,1)} all-gather(bf16[4,3,2,336,8]{3,4,2,1,0:T(8,128)(2,1)S(1)} %bitcast.161), channel_id=1, replica_groups=mesh['cuts_0'=2,'cuts_1'=2,'mode_0'=4,'mode_1'=4,'mode_2'=8] {'mode_2'}, dimensions={0}, use_global_device_ids=true | all-gather | bytes 1161216 | tf_op jit(solution)/shard_map/all_gather | solution.py:20
  82.6 0.0 all-gather.10.cloned.1.call-start
  82.6 13.6 %all-gather.1 = bf16[12,2,344,8]{2,3,1,0:T(8,128)(2,1)S(1)} all-gather(bf16[3,2,344,8]{2,3,1,0:T(8,128)(2,1)S(1)} %get-tuple-element.13), channel_id=3, replica_groups=mesh['cuts_0'=2,'cuts_1'=2,'mode_0'=4,'mode_1'=4,'mode_2'=8] {'mode_1'}, dimensions={0}, use_global_device_ids=true | all-gather | bytes 165120 | tf_op jit(solution)/shard_map/all_gather | solution.py:20
  96.3 13.6 %all_gather.31 = bf16[16,3,2,344,8]{3,4,2,1,0:T(8,128)(2,1)} all-gather(bf16[4,3,2,344,8]{3,4,2,1,0:T(8,128)(2,1)S(1)} %bitcast.162), channel_id=1, replica_groups=mesh['cuts_0'=2,'cuts_1'=2,'mode_0'=4,'mode_1'=4,'mode_2'=8] {'mode_0'}, dimensions={0}, use_global_device_ids=true | all-gather | bytes 660480 | tf_op jit(solution)/shard_map/all_gather | solution.py:20
  109.9 0.0 all-gather.14.cloned.1.call-start
  110.0 0.5 all-gather.14.cloned.1.call-update
  110.5 1.6 copy.70
  112.1 0.8 fusion.46
  112.9 3.7 gather_fusion.1
  116.6 3.7 broadcast_select_fusion.2
  120.4 0.9 copy.45
  121.3 11.7 %all-to-all-start = ((bf16[2,128,8,128]{3,2,0,1:T(8,128)(2,1)}), bf16[2,128,8,128]{3,2,0,1:T(8,128)(2,1)S(1)}, u32[]{:S(2)}, u32[]{:S(2)}) async-start(bf16[2,128,8,128]{3,2,0,1:T(8,128)(2,1)} %copy.45), calls=%async_computation | async-start | bytes 1048576 | tf_op jit(solution)/shard_map/all_to_all | solution.py:69
  133.0 1.4 fusion.47
  136.4 48.8 %all-gather.8.cloned.1.call-done = bf16[128,3,2,336,8]{3,4,2,1,0:T(8,128)(2,1)} async-done(((bf16[32,3,2,336,8]{3,4,2,1,0:T(8,128)(2,1)}), bf16[128,3,2,336,8]{3,4,2,1,0:T(8,128)(2,1)}) %all-gather.8.cloned.1.call-update) | async-done | bytes 4128784 | tf_op jit(solution)/shard_map/all_gather | solution.py:20
  185.1 5.2 copy.41
  190.4 61.7 %all-gather.10.cloned.1.call-done = bf16[128,3,2,344,8]{3,4,2,1,0:T(8,128)(2,1)} async-done(((bf16[16,3,2,344,8]{3,4,2,1,0:T(8,128)(2,1)}), bf16[128,3,2,344,8]{3,4,2,1,0:T(8,128)(2,1)}) %all-gather.10.cloned.1.call-update) | async-done | bytes 4227088 | tf_op jit(solution)/shard_map/all_gather | solution.py:20
  252.0 5.2 copy.42
  257.2 51.9 %all-gather.14.cloned.1.call-done = bf16[128,3,2,344,8]{3,4,2,1,0:T(8,128)(2,1)} async-done(((bf16[32,3,2,344,8]{3,4,2,1,0:T(8,128)(2,1)}), bf16[128,3,2,344,8]{3,4,2,1,0:T(8,128)(2,1)}) %all-gather.14.cloned.1.call-update) | async-done | bytes 4227088 | tf_op jit(solution)/shard_map/all_gather | solution.py:20
  309.1 13.7 %copy_bitcast_fusion = bf16[3,2,1024,1024]{2,3,1,0:T(8,128)(2,1)} fusion(bf16[128,3,2,344,8]{3,4,2,1,0:T(8,128)(2,1)} %all-gather.14.cloned.1.call-done, bf16[128,3,2,344,8]{3,4,2,1,0:T(8,128)(2,1)} %bitcast.153, bf16[128,3,2,336,8]{3,4,2,1,0:T(8,128)(2,1)} %bitcast.152), kind=kLoop, calls=%fused_computation.5 | loop fusion | flops 37748736 | bytes 25165824 | tf_op jit(solution)/shard_map/reshape | solution.py:30
  322.9 2.3 fusion.5
  325.2 2.3 fusion.4
  327.5 2.3 fusion.28
  329.8 2.3 fusion.29
  332.1 0.1 pad_maximum_fusion
  332.2 0.5 copy.48
  332.7 3.7 gather_fusion.2
  336.4 3.7 broadcast_select_fusion.1
  340.2 0.9 copy.49
  341.0 14.8 %all-to-all-start.1 = ((bf16[2,128,8,128]{3,2,0,1:T(8,128)(2,1)}), bf16[2,128,8,128]{3,2,0,1:T(8,128)(2,1)S(1)}, u32[]{:S(2)}, u32[]{:S(2)}) async-start(bf16[2,128,8,128]{3,2,0,1:T(8,128)(2,1)} %copy.49), calls=%async_computation.1 | async-start | bytes 1048576 | tf_op jit(solution)/shard_map/all_to_all | solution.py:69
  357.9 15.8 %all-to-all-done.1 = bf16[2,128,8,128]{3,2,0,1:T(8,128)(2,1)S(1)} async-done(((bf16[2,128,8,128]{3,2,0,1:T(8,128)(2,1)}), bf16[2,128,8,128]{3,2,0,1:T(8,128)(2,1)S(1)}, u32[]{:S(2)}, u32[]{:S(2)}) %all-to-all-start.1) | async-done | bytes 524320 | tf_op jit(solution)/shard_map/all_to_all | solution.py:69
  373.6 2.3 fusion.3
  375.9 2.3 fusion.2
  378.2 2.3 fusion.26
  380.5 2.3 fusion.27
  382.8 0.1 pad_maximum_fusion.1
  382.9 0.5 copy.52
  383.4 3.7 gather_fusion.3
  387.1 3.7 broadcast_select_fusion
  390.9 0.9 copy.53
  391.8 8.2 %all-to-all-start.2 = ((bf16[2,128,8,128]{3,2,0,1:T(8,128)(2,1)}), bf16[2,128,8,128]{3,2,0,1:T(8,128)(2,1)S(1)}, u32[]{:S(2)}, u32[]{:S(2)}) async-start(bf16[2,128,8,128]{3,2,0,1:T(8,128)(2,1)} %copy.53), calls=%async_computation.2 | async-start | bytes 1048576 | tf_op jit(solution)/shard_map/all_to_all | solution.py:69
  401.9 15.7 %all-to-all-done.2 = bf16[2,128,8,128]{3,2,0,1:T(8,128)(2,1)S(1)} async-done(((bf16[2,128,8,128]{3,2,0,1:T(8,128)(2,1)}), bf16[2,128,8,128]{3,2,0,1:T(8,128)(2,1)S(1)}, u32[]{:S(2)}, u32[]{:S(2)}) %all-to-all-start.2) | async-done | bytes 524320 | tf_op jit(solution)/shard_map/all_to_all | solution.py:69
  417.5 2.3 fusion.1
  419.8 2.3 fusion
  422.1 2.3 fusion.24
  424.4 2.3 fusion.25
  426.7 0.8 copy_bitcast_fusion.1
  427.6 0.8 pad_maximum_fusion.2
  428.4 1.2 pad_maximum_fusion.3
  429.6 20.3 %copy.56 = bf16[2,131072]{0,1:T(8,128)(2,1)} copy(bf16[2,131072]{1,0:T(2,128)(2,1)S(1)} %pad_maximum_fusion.3) | data formatting | bytes 1048576 | tf_op jit(solution)/shard_map/stack | solution.py:57
  449.8 21.6 %gather_fusion = bf16[2048,2]{1,0:T(8,128)(2,1)S(1)} fusion(bf16[2,131072]{0,1:T(8,128)(2,1)} %copy.56, s32[2048]{0:T(1024)S(1)} %broadcast_clamp_fusion), kind=kCustom, calls=%fused_computation.3 | custom fusion | bytes 24576 | tf_op jit(solution)/shard_map/jit(_take)/gather | solution.py:79
  471.5 0.7 select_bitcast_fusion
  472.2 28.2 %psum.35 = f32[2,2048]{0,1:T(8,128)S(1)} all-reduce(f32[2,2048]{0,1:T(8,128)S(1)} %select_bitcast_fusion), channel_id=1, replica_groups=mesh['cuts_0'=2,'cuts_1'=2,'mode_0'=4,'mode_1'=4,'mode_2'=8] {'cuts_0'}, use_global_device_ids=true, to_apply=%region_0.0 | all-reduce | flops 4096 | bytes 32768 | tf_op jit(solution)/shard_map/psum | solution.py:45
  500.5 5.7 psum.36
  506.1 44.0 %psum.37 = f32[2,2048]{0,1:T(8,128)S(1)} all-reduce(f32[2,2048]{0,1:T(8,128)S(1)} %psum.36), channel_id=1, replica_groups=mesh['cuts_0'=2,'cuts_1'=2,'mode_0'=4,'mode_1'=4,'mode_2'=8] {'mode_0'}, use_global_device_ids=true, to_apply=%region_2.4 | all-reduce | flops 4096 | bytes 32768 | tf_op jit(solution)/shard_map/psum | solution.py:45
  550.2 53.7 %psum.38 = f32[2,2048]{0,1:T(8,128)S(1)} all-reduce(f32[2,2048]{0,1:T(8,128)S(1)} %psum.37), channel_id=1, replica_groups=mesh['cuts_0'=2,'cuts_1'=2,'mode_0'=4,'mode_1'=4,'mode_2'=8] {'mode_1'}, use_global_device_ids=true, to_apply=%region_3.5 | all-reduce | flops 4096 | bytes 32768 | tf_op jit(solution)/shard_map/psum | solution.py:45
  603.9 60.6 %psum.39 = f32[2,2048]{0,1:T(8,128)S(1)} all-reduce(f32[2,2048]{0,1:T(8,128)S(1)} %psum.38), channel_id=1, replica_groups=mesh['cuts_0'=2,'cuts_1'=2,'mode_0'=4,'mode_1'=4,'mode_2'=8] {'mode_2'}, use_global_device_ids=true, to_apply=%region_4.6 | all-reduce | flops 4096 | bytes 32768 | tf_op jit(solution)/shard_map/psum | solution.py:45
  664.6 0.6 copy.57
  (17 shorter events, 0.2 us)
Async XLA Ops:
  7.2 102.8 %all-gather.12.cloned.1.call-start = ((), (), s32[]{:S(2)}) async-start(), calls=%async_computation.5 | async-start | bytes 1474560 | tf_op jit(solution)/shard_map/all_gather | solution.py:20
  41.6 143.6 %all-gather.8.cloned.1.call-start = ((), (), s32[]{:S(2)}) async-start(), calls=%async_computation.3 | async-start | bytes 5898240 | tf_op jit(solution)/shard_map/all_gather | solution.py:20
  82.6 169.5 %all-gather.10.cloned.1.call-start = ((), (), s32[]{:S(2)}) async-start(), calls=%async_computation.4 | async-start | bytes 5308416 | tf_op jit(solution)/shard_map/all_gather | solution.py:20
  109.9 199.2 %all-gather.14.cloned.1.call-start = ((), (), s32[]{:S(2)}) async-start(), calls=%async_computation.6 | async-start | bytes 5898240 | tf_op jit(solution)/shard_map/all_gather | solution.py:20
  121.3 201.6 %all-to-all-start = ((bf16[2,128,8,128]{3,2,0,1:T(8,128)(2,1)}), bf16[2,128,8,128]{3,2,0,1:T(8,128)(2,1)S(1)}, u32[]{:S(2)}, u32[]{:S(2)}) async-start(bf16[2,128,8,128]{3,2,0,1:T(8,128)(2,1)} %copy.45), calls=%async_computation | async-start | bytes 1048576 | tf_op jit(solution)/shard_map/all_to_all | solution.py:69
  332.1 69.7 %copy-start = (s32[2048]{0:T(1024)S(1)}, s32[2048]{0:T(1024)}, u32[]{:S(2)}) copy-start(s32[2048]{0:T(1024)} %param.13) | copy-start | bytes 24580
  332.1 69.7 %copy-start.1 = (s32[2048]{0:T(1024)S(1)}, s32[2048]{0:T(1024)}, u32[]{:S(2)}) copy-start(s32[2048]{0:T(1024)} %param.12) | copy-start | bytes 24580
  341.0 32.6 %all-to-all-start.1 = ((bf16[2,128,8,128]{3,2,0,1:T(8,128)(2,1)}), bf16[2,128,8,128]{3,2,0,1:T(8,128)(2,1)S(1)}, u32[]{:S(2)}, u32[]{:S(2)}) async-start(bf16[2,128,8,128]{3,2,0,1:T(8,128)(2,1)} %copy.49), calls=%async_computation.1 | async-start | bytes 1048576 | tf_op jit(solution)/shard_map/all_to_all | solution.py:69
  391.8 25.8 %all-to-all-start.2 = ((bf16[2,128,8,128]{3,2,0,1:T(8,128)(2,1)}), bf16[2,128,8,128]{3,2,0,1:T(8,128)(2,1)S(1)}, u32[]{:S(2)}, u32[]{:S(2)}) async-start(bf16[2,128,8,128]{3,2,0,1:T(8,128)(2,1)} %copy.53), calls=%async_computation.2 | async-start | bytes 1048576 | tf_op jit(solution)/shard_map/all_to_all | solution.py:69
Sparse Core Ops, SparseCore 0:
  41.7 36.6 all-gather.11
  82.7 102.4 all-gather.7
  187.2 64.7 all-gather.9
  254.0 55.1 all-gather.13
where the time goes:
time: 673 us; the launch traced here: 672 us
  blocking collectives  293 us (44%)
  waiting for transfers between devices  194 us (29%)
  local copies, waits for them, and re-layouts  74.1 us (11%)
  starting transfers between devices  34.8 us (5%)
  other arithmetic  27.9 us (4%)
  matrix products  27.6 us (4%)
  between operations  19.9 us (3%)
    psum x5, blocking collectives, over_axes(): shard = lax.psum(shard, axis)  192 us
    all_gather x4, waiting for transfers between devices, gather_in_order(): blocks = lax.all_gather(blocks, axes[k], axis=0, tiled=True)  162 us
    all_gather x5, blocking collectives, gather_in_order(): blocks = lax.all_gather(blocks, axes[k], axis=0, tiled=True)  101 us
    all_to_all x3, starting transfers between devices, body(): lax.all_to_all(view, MODE, split_axis=1, concat_axis=1, tiled=True)  34.7 us
    all_to_all x3, waiting for transfers between devices, body(): lax.all_to_all(view, MODE, split_axis=1, concat_axis=1, tiled=True)  31.4 us
    dot_general x12, matrix products, product(): lax.dot_general(left, right, numbers, preferred_element_type=jnp.float32)  27.6 us
    another operation x4, local copies, waits for them, and re-layouts, absorb(): return jnp.stack([real, imag], axis=0)  22.1 us
    gather x1, local copies, waits for them, and re-layouts, body(): values = jnp.take(flat, flat_index, axis=1).astype(jnp.float32)  21.6 us
  transfers between devices with their start and end apart: 7, of which 5 were waited for; matrix products, arithmetic and copies ran while one was open for 6% of the time, Pallas kernels for 0%

commit v1 on v0

--- a/solution.py
+++ b/solution.py
@@ -17,7 +17,9 @@
 def gather_in_order(shard, axes, turns):
     blocks = shard[None]
     for k in turns:
-        blocks = lax.all_gather(blocks, axes[k], axis=0, tiled=True)
+        blocks = jnp.concatenate(
+            lax.all_to_all(jnp.stack([blocks] * lax.axis_size(axes[k])), axes[k], 0, 0), axis=0
+        )
     held = [lax.axis_size(axes[k]) for k in reversed(turns)]
     blocks = blocks.reshape(*held, *shard.shape)
     turned = sorted(range(len(turns)), key=lambda place: turns[len(turns) - 1 - place])

time: 673 us -> 748 us (1.11)
  the two profiles are of different devices: /device:TPU:4 before, /device:TPU:2 now
where the time goes in v1:
time: 748 us; the launch traced here: 746 us
  blocking collectives  448 us (60%)
  waiting for transfers between devices  124 us (17%)
  local copies, waits for them, and re-layouts  71.7 us (10%)
  starting transfers between devices  44.7 us (6%)
  matrix products  27.6 us (4%)
  other arithmetic  23.6 us (3%)
    all_to_all x7, blocking collectives, gather_in_order(): lax.all_to_all(jnp.stack([blocks] * lax.axis_size(axes[k])), axes[k], 0, 0)  255 us
    psum x5, blocking collectives, over_axes(): shard = lax.psum(shard, axis)  192 us
    all_to_all x2, waiting for transfers between devices, gather_in_order(): lax.all_to_all(jnp.stack([blocks] * lax.axis_size(axes[k])), axes[k], 0, 0)  94.2 us
    all_to_all x3, starting transfers between devices, body(): lax.all_to_all(view, MODE, split_axis=1, concat_axis=1, tiled=True)  30.5 us
    all_to_all x3, waiting for transfers between devices, body(): lax.all_to_all(view, MODE, split_axis=1, concat_axis=1, tiled=True)  29.7 us
    dot_general x12, matrix products, product(): lax.dot_general(left, right, numbers, preferred_element_type=jnp.float32)  27.6 us
    another operation x4, local copies, waits for them, and re-layouts, absorb(): return jnp.stack([real, imag], axis=0)  22.1 us
    gather x1, local copies, waits for them, and re-layouts, body(): values = jnp.take(flat, flat_index, axis=1).astype(jnp.float32)  21.6 us
  transfers between devices with their start and end apart: 5, of which 4 were waited for; matrix products, arithmetic and copies ran while one was open for 4% of the time, Pallas kernels for 0%

profile of v1, /device:TPU:2, one launch (start us, length us, event | category | flops | bytes accessed | tf_op | source)
XLA Modules:
  0.0 746.1 jit_solution(7715536987216209826)
XLA Ops:
  0.6 0.8 split.9
  1.4 0.7 stack.66
  2.1 9.2 %all-to-all-start = ((bf16[4,1,3,2,336,8]{4,5,3,2,1,0:T(8,128)(2,1)}), bf16[4,1,3,2,336,8]{4,5,3,2,1,0:T(8,128)(2,1)S(1)}, u32[]{:S(2)}, u32[]{:S(2)}) async-start(bf16[4,1,3,2,336,8]{4,5,3,2,1,0:T(8,128)(2,1)} %stack.66), calls=%async_computation | async-start | bytes 294912 | tf_op jit(solution)/shard_map/all_to_all | solution.py:21
  11.3 0.9 fusion.45
  12.2 3.7 all-to-all-done
  15.9 9.0 %all_to_all.60 = bf16[4,1,3,2,344,8]{4,5,3,2,1,0:T(8,128)(2,1)S(1)} all-to-all(bf16[4,1,3,2,344,8]{4,5,3,2,1,0:T(8,128)(2,1)S(1)} %stack.69), channel_id=1, replica_groups=mesh['cuts_0'=2,'cuts_1'=2,'mode_0'=4,'mode_1'=4,'mode_2'=8] {'mode_1'}, dimensions={0} | all-to-all | bytes 264192 | tf_op jit(solution)/shard_map/all_to_all | solution.py:21
  24.9 18.9 %all_to_all.61 = bf16[8,1,3,2,344,8]{4,5,3,2,1,0:T(8,128)(2,1)S(1)} all-to-all(bf16[8,1,3,2,344,8]{4,5,3,2,1,0:T(8,128)(2,1)S(1)} %stack.72), channel_id=1, replica_groups=mesh['cuts_0'=2,'cuts_1'=2,'mode_0'=4,'mode_1'=4,'mode_2'=8] {'mode_2'}, dimensions={0} | all-to-all | bytes 528384 | tf_op jit(solution)/shard_map/all_to_all | solution.py:21
  43.9 10.8 %all_to_all.62 = bf16[4,4,3,2,344,8]{4,5,3,2,1,0:T(8,128)(2,1)S(1)} all-to-all(bf16[4,4,3,2,344,8]{4,5,3,2,1,0:T(8,128)(2,1)S(1)} %stack.70), channel_id=1, replica_groups=mesh['cuts_0'=2,'cuts_1'=2,'mode_0'=4,'mode_1'=4,'mode_2'=8] {'mode_0'}, dimensions={0} | all-to-all | bytes 1056768 | tf_op jit(solution)/shard_map/all_to_all | solution.py:21
  54.7 0.1 stack.67
  54.8 28.9 %all_to_all.63 = bf16[8,4,3,2,336,8]{4,5,3,2,1,0:T(8,128)(2,1)S(1)} all-to-all(bf16[8,4,3,2,336,8]{4,5,3,2,1,0:T(8,128)(2,1)S(1)} %stack.67), channel_id=1, replica_groups=mesh['cuts_0'=2,'cuts_1'=2,'mode_0'=4,'mode_1'=4,'mode_2'=8] {'mode_2'}, dimensions={0} | all-to-all | bytes 2064384 | tf_op jit(solution)/shard_map/all_to_all | solution.py:21
  83.7 0.1 stack.73
  83.8 24.6 %all_to_all.64 = bf16[4,8,3,2,344,8]{4,5,3,2,1,0:T(8,128)(2,1)S(1)} all-to-all(bf16[4,8,3,2,344,8]{4,5,3,2,1,0:T(8,128)(2,1)S(1)} %stack.73), channel_id=1, replica_groups=mesh['cuts_0'=2,'cuts_1'=2,'mode_0'=4,'mode_1'=4,'mode_2'=8] {'mode_1'}, dimensions={0} | all-to-all | bytes 2113536 | tf_op jit(solution)/shard_map/all_to_all | solution.py:21
  108.4 0.4 stack.74
  108.8 54.9 %all_to_all.65 = bf16[4,32,3,2,344,8]{4,5,3,2,1,0:T(8,128)(2,1)} all-to-all(bf16[4,32,3,2,344,8]{4,5,3,2,1,0:T(8,128)(2,1)S(1)} %stack.74), channel_id=1, replica_groups=mesh['cuts_0'=2,'cuts_1'=2,'mode_0'=4,'mode_1'=4,'mode_2'=8] {'mode_0'}, dimensions={0} | all-to-all | bytes 8454144 | tf_op jit(solution)/shard_map/all_to_all | solution.py:21
  163.8 0.4 stack.71
  164.2 108.2 %all_to_all.66 = bf16[8,16,3,2,344,8]{4,5,3,2,1,0:T(8,128)(2,1)} all-to-all(bf16[8,16,3,2,344,8]{4,5,3,2,1,0:T(8,128)(2,1)S(1)} %stack.71), channel_id=1, replica_groups=mesh['cuts_0'=2,'cuts_1'=2,'mode_0'=4,'mode_1'=4,'mode_2'=8] {'mode_2'}, dimensions={0} | all-to-all | bytes 8454144 | tf_op jit(solution)/shard_map/all_to_all | solution.py:21
  272.4 2.5 stack.68
  274.9 5.1 all-to-all-start.2
  280.0 0.5 copy.62
  280.6 3.7 gather_fusion.1
  284.3 3.7 broadcast_select_fusion.2
  288.1 0.9 copy.37
  289.0 90.5 %all-to-all-done.2 = bf16[4,32,3,2,336,8]{4,5,3,2,1,0:T(8,128)(2,1)} async-done(((bf16[4,32,3,2,336,8]{4,5,3,2,1,0:T(8,128)(2,1)}), bf16[4,32,3,2,336,8]{4,5,3,2,1,0:T(8,128)(2,1)}, u32[]{:S(2)}, u32[]{:S(2)}) %all-to-all-start.2) | async-done | bytes 4128800 | tf_op jit(solution)/shard_map/all_to_all | solution.py:21
  379.4 8.3 %all-to-all-start.9 = ((bf16[2,128,8,128]{3,2,0,1:T(8,128)(2,1)}), bf16[2,128,8,128]{3,2,0,1:T(8,128)(2,1)S(1)}, u32[]{:S(2)}, u32[]{:S(2)}) async-start(bf16[2,128,8,128]{3,2,0,1:T(8,128)(2,1)} %copy.37), calls=%async_computation.9 | async-start | bytes 1048576 | tf_op jit(solution)/shard_map/all_to_all | solution.py:71
  387.7 0.7 fusion.47
  390.3 3.2 copy.34
  393.5 3.1 copy.33
  396.7 9.4 %copy_bitcast_fusion = bf16[3,2,1024,1024]{2,3,1,0:T(8,128)(2,1)} fusion(bf16[128,3,2,344,8]{3,4,2,1,0:T(8,128)(2,1)S(1)} %bitcast.158, bf16[128,3,2,344,8]{3,4,2,1,0:T(8,128)(2,1)S(1)} %bitcast.159, bf16[128,3,2,336,8]{3,4,2,1,0:T(8,128)(2,1)S(1)} %bitcast.160), kind=kLoop, calls=%fused_computation.5 | loop fusion | flops 37748736 | bytes 25165824 | tf_op jit(solution)/shard_map/reshape | solution.py:32
  406.2 2.3 fusion.5
  408.4 2.3 fusion.4
  410.8 2.3 fusion.28
  413.1 2.3 fusion.29
  415.4 0.5 copy.40
  416.0 3.7 gather_fusion.2
  419.7 3.7 broadcast_select_fusion.1
  423.4 0.9 copy.41
  424.3 14.2 %all-to-all-start.10 = ((bf16[2,128,8,128]{3,2,0,1:T(8,128)(2,1)}), bf16[2,128,8,128]{3,2,0,1:T(8,128)(2,1)S(1)}, u32[]{:S(2)}, u32[]{:S(2)}) async-start(bf16[2,128,8,128]{3,2,0,1:T(8,128)(2,1)} %copy.41), calls=%async_computation.10 | async-start | bytes 1048576 | tf_op jit(solution)/shard_map/all_to_all | solution.py:71
  440.6 13.9 %all-to-all-done.10 = bf16[2,128,8,128]{3,2,0,1:T(8,128)(2,1)S(1)} async-done(((bf16[2,128,8,128]{3,2,0,1:T(8,128)(2,1)}), bf16[2,128,8,128]{3,2,0,1:T(8,128)(2,1)S(1)}, u32[]{:S(2)}, u32[]{:S(2)}) %all-to-all-start.10) | async-done | bytes 524320 | tf_op jit(solution)/shard_map/all_to_all | solution.py:71
  454.4 2.3 fusion.3
  456.7 2.3 fusion.2
  459.0 2.3 fusion.26
  461.4 2.3 fusion.27
  463.7 0.5 copy.44
  464.3 3.7 gather_fusion.3
  468.0 3.7 broadcast_select_fusion
  471.7 0.9 copy.45
  472.6 8.1 %all-to-all-start.11 = ((bf16[2,128,8,128]{3,2,0,1:T(8,128)(2,1)}), bf16[2,128,8,128]{3,2,0,1:T(8,128)(2,1)S(1)}, u32[]{:S(2)}, u32[]{:S(2)}) async-start(bf16[2,128,8,128]{3,2,0,1:T(8,128)(2,1)} %copy.45), calls=%async_computation.11 | async-start | bytes 1048576 | tf_op jit(solution)/shard_map/all_to_all | solution.py:71
  482.7 15.8 %all-to-all-done.11 = bf16[2,128,8,128]{3,2,0,1:T(8,128)(2,1)S(1)} async-done(((bf16[2,128,8,128]{3,2,0,1:T(8,128)(2,1)}), bf16[2,128,8,128]{3,2,0,1:T(8,128)(2,1)S(1)}, u32[]{:S(2)}, u32[]{:S(2)}) %all-to-all-start.11) | async-done | bytes 524320 | tf_op jit(solution)/shard_map/all_to_all | solution.py:71
  498.5 2.3 fusion.1
  500.8 2.3 fusion
  503.1 2.3 fusion.24
  505.4 2.3 fusion.25
  507.7 0.8 copy_bitcast_fusion.1
  508.5 0.8 pad_maximum_fusion.2
  509.4 1.2 pad_maximum_fusion.3
  510.6 20.2 %copy.48 = bf16[2,131072]{0,1:T(8,128)(2,1)} copy(bf16[2,131072]{1,0:T(2,128)(2,1)S(1)} %pad_maximum_fusion.3) | data formatting | bytes 1048576 | tf_op jit(solution)/shard_map/stack | solution.py:59
  530.8 21.6 %gather_fusion = bf16[2048,2]{1,0:T(8,128)(2,1)S(1)} fusion(bf16[2,131072]{0,1:T(8,128)(2,1)} %copy.48, s32[2048]{0:T(1024)S(1)} %broadcast_clamp_fusion), kind=kCustom, calls=%fused_computation.3 | custom fusion | bytes 24576 | tf_op jit(solution)/shard_map/jit(_take)/gather | solution.py:81
  552.4 0.7 select_bitcast_fusion
  553.1 42.6 %psum.35 = f32[2,2048]{0,1:T(8,128)S(1)} all-reduce(f32[2,2048]{0,1:T(8,128)S(1)} %select_bitcast_fusion), channel_id=1, replica_groups=mesh['cuts_0'=2,'cuts_1'=2,'mode_0'=4,'mode_1'=4,'mode_2'=8] {'cuts_0'}, use_global_device_ids=true, to_apply=%region_0.0 | all-reduce | flops 4096 | bytes 32768 | tf_op jit(solution)/shard_map/psum | solution.py:47
  595.8 5.7 psum.36
  601.5 31.2 %psum.37 = f32[2,2048]{0,1:T(8,128)S(1)} all-reduce(f32[2,2048]{0,1:T(8,128)S(1)} %psum.36), channel_id=1, replica_groups=mesh['cuts_0'=2,'cuts_1'=2,'mode_0'=4,'mode_1'=4,'mode_2'=8] {'mode_0'}, use_global_device_ids=true, to_apply=%region_2.4 | all-reduce | flops 4096 | bytes 32768 | tf_op jit(solution)/shard_map/psum | solution.py:47
  632.6 53.0 %psum.38 = f32[2,2048]{0,1:T(8,128)S(1)} all-reduce(f32[2,2048]{0,1:T(8,128)S(1)} %psum.37), channel_id=1, replica_groups=mesh['cuts_0'=2,'cuts_1'=2,'mode_0'=4,'mode_1'=4,'mode_2'=8] {'mode_1'}, use_global_device_ids=true, to_apply=%region_3.5 | all-reduce | flops 4096 | bytes 32768 | tf_op jit(solution)/shard_map/psum | solution.py:47
  685.6 59.7 %psum.39 = f32[2,2048]{0,1:T(8,128)S(1)} all-reduce(f32[2,2048]{0,1:T(8,128)S(1)} %psum.38), channel_id=1, replica_groups=mesh['cuts_0'=2,'cuts_1'=2,'mode_0'=4,'mode_1'=4,'mode_2'=8] {'mode_2'}, use_global_device_ids=true, to_apply=%region_4.6 | all-reduce | flops 4096 | bytes 32768 | tf_op jit(solution)/shard_map/psum | solution.py:47
  745.4 0.6 copy.49
  (31 shorter events, 0.3 us)
Async XLA Ops:
  2.1 13.8 %all-to-all-start = ((bf16[4,1,3,2,336,8]{4,5,3,2,1,0:T(8,128)(2,1)}), bf16[4,1,3,2,336,8]{4,5,3,2,1,0:T(8,128)(2,1)S(1)}, u32[]{:S(2)}, u32[]{:S(2)}) async-start(bf16[4,1,3,2,336,8]{4,5,3,2,1,0:T(8,128)(2,1)} %stack.66), calls=%async_computation | async-start | bytes 294912 | tf_op jit(solution)/shard_map/all_to_all | solution.py:21
  274.9 5.1 copy-start
  274.9 5.7 copy-start.3
  274.9 104.5 %all-to-all-start.2 = ((bf16[4,32,3,2,336,8]{4,5,3,2,1,0:T(8,128)(2,1)}), bf16[4,32,3,2,336,8]{4,5,3,2,1,0:T(8,128)(2,1)}, u32[]{:S(2)}, u32[]{:S(2)}) async-start(bf16[4,32,3,2,336,8]{4,5,3,2,1,0:T(8,128)(2,1)} %stack.68), calls=%async_computation.2 | async-start | bytes 9437184 | tf_op jit(solution)/shard_map/all_to_all | solution.py:21
  280.0 107.7 %copy-start.4 = (s32[3]{0:T(128)S(1)}, s32[3]{0:T(128)}, u32[]{:S(2)}) copy-start(s32[3]{0:T(128)} %param.10) | copy-start | bytes 40
  379.4 26.7 %all-to-all-start.9 = ((bf16[2,128,8,128]{3,2,0,1:T(8,128)(2,1)}), bf16[2,128,8,128]{3,2,0,1:T(8,128)(2,1)S(1)}, u32[]{:S(2)}, u32[]{:S(2)}) async-start(bf16[2,128,8,128]{3,2,0,1:T(8,128)(2,1)} %copy.37), calls=%async_computation.9 | async-start | bytes 1048576 | tf_op jit(solution)/shard_map/all_to_all | solution.py:71
  390.3 6.4 slice-start
  393.5 3.2 slice-start.1
  424.3 30.1 %all-to-all-start.10 = ((bf16[2,128,8,128]{3,2,0,1:T(8,128)(2,1)}), bf16[2,128,8,128]{3,2,0,1:T(8,128)(2,1)S(1)}, u32[]{:S(2)}, u32[]{:S(2)}) async-start(bf16[2,128,8,128]{3,2,0,1:T(8,128)(2,1)} %copy.41), calls=%async_computation.10 | async-start | bytes 1048576 | tf_op jit(solution)/shard_map/all_to_all | solution.py:71
  461.3 21.3 %copy-start.1 = (s32[2048]{0:T(1024)S(1)}, s32[2048]{0:T(1024)}, u32[]{:S(2)}) copy-start(s32[2048]{0:T(1024)} %param.13) | copy-start | bytes 24580
  461.4 21.3 %copy-start.2 = (s32[2048]{0:T(1024)S(1)}, s32[2048]{0:T(1024)}, u32[]{:S(2)}) copy-start(s32[2048]{0:T(1024)} %param.12) | copy-start | bytes 24580
  472.6 25.9 %all-to-all-start.11 = ((bf16[2,128,8,128]{3,2,0,1:T(8,128)(2,1)}), bf16[2,128,8,128]{3,2,0,1:T(8,128)(2,1)S(1)}, u32[]{:S(2)}, u32[]{:S(2)}) async-start(bf16[2,128,8,128]{3,2,0,1:T(8,128)(2,1)} %copy.45), calls=%async_computation.11 | async-start | bytes 1048576 | tf_op jit(solution)/shard_map/all_to_all | solution.py:71
